TPU v7x, 1024 devices: a whole 4x4x32 slice. The times are simulated.
1024 devices in a mesh: row: 32 (over z), col: 32 (over y, x, core).
Axes of the slice: x: 4, y: 4, z: 32, core: 2. Of those that a mesh axis runs over, the one named last changes fastest.
Arguments:
- momentum: float32 [8192, 28672], P('row', 'col'), may hold values from -400 to 400, as said below
- gradient: bfloat16 [8192, 28672], P('row', 'col'), may hold values from -3 to 3
- right_prev: float32 [28672, 256], P('col'), may hold values from -5 to 5
Outputs:
- new_momentum: float32 [8192, 28672], P('row', 'col')
- right_next: float32 [28672, 256], P('col')
- update: bfloat16 [8192, 28672], P('row', 'col')
Inputs may be any that keep to these rules, and one draw needn't show every extreme that they name: momentum entries are finite reals.
All inputs are finite; a program needn't handle non-finite values.
Results may differ from a plain program's by a relative error of at most 0.001.
Values sent between devices are 32-bit elements; how exact they have to be, the bound alone decides.
No kernel may reach another device: no remote copies, remote signals or barrier semaphores. Data moves between devices by JAX's collectives and lax.ppermute only.
A program may use at most 32 MiB of HBM per device.

v0:
```python
import jax
import jax.numpy as jnp
from jax import lax
from jax.sharding import PartitionSpec as P

D = 8192
FF = 28672
RANK = 256


HI = lax.Precision.HIGHEST


def orthogonal(left, gram):
    chol = jnp.linalg.cholesky(gram)
    return jax.scipy.linalg.solve_triangular(chol, left.T, lower=True).T


def on_device(momentum, gradient, right_prev):
    merged = momentum + gradient.astype(jnp.float32)
    partial_value = jnp.dot(merged, right_prev, precision=HI, preferred_element_type=jnp.float32)
    left = lax.psum(partial_value, "col")
    gram = lax.psum(jnp.dot(left.T, left, precision=HI, preferred_element_type=jnp.float32), "row")
    ortho = orthogonal(left, gram)
    local_right = jnp.dot(merged.T, ortho, precision=HI, preferred_element_type=jnp.float32)
    right = lax.psum(local_right, "row")
    colsq = lax.psum(jnp.sum(right * right, axis=0), "col")
    right_next = right * lax.rsqrt(colsq / FF + 1e-06)
    new_momentum = merged - 0.05 * jnp.dot(
        ortho, right.T, precision=HI, preferred_element_type=jnp.float32
    )
    factor = jnp.sqrt(jnp.float32(D) / jnp.float32(RANK))
    update = (
        factor * jnp.dot(ortho, right_next.T, precision=HI, preferred_element_type=jnp.float32)
    ).astype(jnp.bfloat16)
    return (new_momentum, right_next, update)


def solution(mesh):
    in_specs = (P("row", "col"), P("row", "col"), P("col", None))
    out_specs = (P("row", "col"), P("col", None), P("row", "col"))
    return jax.shard_map(
        on_device, mesh=mesh, in_specs=in_specs, out_specs=out_specs, check_vma=False
    )
```

profile of v0, /device:TPU:1, one launch (start us, length us, event | category | flops | bytes accessed | tf_op | source)
XLA Modules:
  0.0 862.8 jit_solution(14807542863643629155)
XLA Ops:
  7.2 1.1 copy-done
  8.3 3.0 fusion.3
  11.5 182.9 %all-reduce.5.cloned.1.call-done = f32[256,256]{1,0:T(8,128)} async-done(((f32[256,256]{1,0:T(8,128)}), f32[256,256]{1,0:T(8,128)}) %all-reduce.5.cloned.1.call-update) | async-done | bytes 262160 | tf_op jit(solution)/shard_map/psum | solution.py:22
  194.3 2.3 fusion.16
  196.8 246.1 %all-reduce.7.cloned.1.call-done = f32[256,256]{0,1:T(8,128)} async-done(((f32[256,256]{0,1:T(8,128)}), f32[256,256]{0,1:T(8,128)}) %all-reduce.7.cloned.1.call-update) | async-done | bytes 262160 | tf_op jit(solution)/shard_map/psum | solution.py:23
  442.9 1.1 copy.7
  444.1 11.7 %cholesky.50 = f32[128,128]{1,0:T(8,128)S(1)} custom-call(f32[128,128]{1,0:T(8,128)S(1)} %cholesky.118), custom_call_target="Cholesky" | custom-call | tf_op jit(solution)/shard_map/jit(cholesky)/cholesky | solution.py:15
  455.9 9.8 %custom-call.15 = f32[1,128,128]{1,2,0:T(8,128)S(1)} custom-call(f32[1,128,128]{2,1,0:T(8,128)S(1)} %get-tuple-element.24), custom_call_target="InvertDiagBlocksLowerTriangular" | custom-call | tf_op jit(solution)/shard_map/jit(cholesky)/cholesky | solution.py:15
  466.2 11.7 %cholesky.105 = f32[128,128]{1,0:T(8,128)S(1)} custom-call(f32[128,128]{1,0:T(8,128)S(1)} %convolution_subtract_fusion.1), custom_call_target="Cholesky" | custom-call | tf_op jit(solution)/shard_map/jit(cholesky)/cholesky | solution.py:15
  478.0 0.6 compare_reduce_fusion
  480.0 4.1 while.1
  480.2 0.6 fusion.27
  480.8 1.4 bitcast_dynamic-update-slice_fusion.2
  482.2 0.6 fusion.27
  482.8 1.4 bitcast_dynamic-update-slice_fusion.2
  484.2 19.7 %custom-call.16 = f32[2,128,128]{1,2,0:T(8,128)S(1)} custom-call(f32[2,128,128]{2,1,0:T(8,128)S(1)} %get-tuple-element.10), custom_call_target="InvertDiagBlocksLowerTriangular" | custom-call | tf_op jit(solution)/shard_map/jit(_solve_triangular)/triangular_solve | solution.py:16
  504.2 0.4 convolution_subtract_fusion
  504.6 0.3 fusion.8
  504.9 2.5 fusion.2
  507.5 258.7 %all-reduce.9.cloned.1.call-done = f32[896,256]{1,0:T(8,128)} async-done(((f32[896,256]{1,0:T(8,128)}), f32[896,256]{1,0:T(8,128)}) %all-reduce.9.cloned.1.call-update) | async-done | bytes 917520 | tf_op jit(solution)/shard_map/psum | solution.py:26
  766.1 1.4 multiply_reduce_fusion
  767.5 83.4 %psum.31 = f32[256]{0:T(256)S(1)} all-reduce(f32[256]{0:T(256)S(1)} %multiply_reduce_fusion), channel_id=1, replica_groups=mesh['row'=32,'col'=32] {'col'}, use_global_device_ids=true, to_apply=%region_8.9 | all-reduce | flops 256 | bytes 2048 | tf_op jit(solution)/shard_map/psum | solution.py:27
  851.0 2.6 fusion.1
  853.6 2.7 fusion
  (35 shorter events, 1.3 us)
Async XLA Ops:
  7.2 1.2 copy-start
  7.2 187.2 %all-reduce.5.cloned.1.call-start = ((), (), s32[]{:S(2)}) async-start(), calls=%async_computation | async-start | bytes 524288 | tf_op jit(solution)/shard_map/psum | solution.py:22
  11.4 431.5 %all-reduce.7.cloned.1.call-start = ((), (), s32[]{:S(2)}) async-start(), calls=%async_computation.1 | async-start | bytes 524288 | tf_op jit(solution)/shard_map/psum | solution.py:23
  196.7 569.4 %all-reduce.9.cloned.1.call-start = ((), (), s32[]{:S(2)}) async-start(), calls=%async_computation.2 | async-start | bytes 1835008 | tf_op jit(solution)/shard_map/psum | solution.py:26
  442.9 1.2 copy-start.6
  477.9 25.9 %copy-start.5 = (f32[256,256]{1,0:T(8,128)S(1)}, f32[256,256]{1,0:T(8,128)}, u32[]{:S(2)}) copy-start(f32[256,256]{1,0:T(8,128)} %all-reduce.5.cloned.1.call-done) | copy-start | bytes 786436
  479.9 25.0 %copy-start.3 = (bf16[256,896]{1,0:T(8,128)(2,1)S(1)}, bf16[256,896]{1,0:T(8,128)(2,1)}, u32[]{:S(2)}) copy-start(bf16[256,896]{1,0:T(8,128)(2,1)} %param.4) | copy-start | bytes 1376260
  480.0 24.9 %copy-start.1 = (f32[256,896]{1,0:T(8,128)S(1)}, f32[256,896]{1,0:T(8,128)}, u32[]{:S(2)}) copy-start(f32[256,896]{1,0:T(8,128)} %param.3) | copy-start | bytes 2752516
  766.1 84.8 %copy-start.2 = (f32[896,256]{1,0:T(8,128)S(1)}, f32[896,256]{1,0:T(8,128)}, u32[]{:S(2)}) copy-start(f32[896,256]{1,0:T(8,128)} %all-reduce.9.cloned.1.call-done) | copy-start | bytes 2752516
  851.0 5.3 copy-start.4
Sparse Core Ops, SparseCore 0:
  11.8 182.5 all-reduce.4
  197.2 245.6 all-reduce.6
  507.6 258.5 all-reduce.8
where the time goes:
time: 863 us
  waiting for transfers between devices  688 us (80%)
  blocking collectives  83.4 us (10%)
  other arithmetic  55.2 us (6%)
  between operations  15.2 us (2%)
  matrix products  14.7 us (2%)
    psum x1, waiting for transfers between devices, on_device(): right = lax.psum(local_right, 'row')  259 us
    psum x1, waiting for transfers between devices, on_device(): lax.psum(jnp.dot(left.T, left, precision=HI, preferred_element_type=jnp.f...  246 us
    psum x1, waiting for transfers between devices, on_device(): left = lax.psum(partial_value, 'col')  183 us
    psum x1, blocking collectives, on_device(): colsq = lax.psum(jnp.sum(right * right, axis=0), 'col')  83.4 us
    another operation x6, other arithmetic, orthogonal(): chol = jnp.linalg.cholesky(gram)  33.9 us
    another operation x3, other arithmetic, orthogonal(): return jax.scipy.linalg.solve_triangular(chol, left.T, lower=True).T  19.7 us
  transfers between devices with their start and end apart: 3, of which 3 were waited for; matrix products, arithmetic and copies ran while one was open for 0% of the time, Pallas kernels for 0%

commit v1 on v0

v1 whole, which is shorter than its diff:
```python
import jax
import jax.numpy as jnp
from jax import lax
from jax.sharding import Mesh, PartitionSpec as P

HI = lax.Precision.HIGHEST
NEAR = 4
FAR_AXIS, NEAR_AXIS, COL = "far", "near", "col"


def dot(a, b, contract):
    return lax.dot_general(
        a, b, ((contract[:1], contract[1:]), ((), ())), precision=HI, preferred_element_type=jnp.float32
    )


def exchange(blocks, axis):
    return lax.all_to_all(blocks, axis, 0, 0)


def on_device(far, cols, momentum, gradient, right_prev):
    near = NEAR
    rows, width = momentum.shape
    rank = right_prev.shape[1]
    depth, full_width = far * near * rows, cols * width
    step, part = rank // (far * near), rank // cols
    merged = momentum + gradient.astype(jnp.float32)

    local = dot(right_prev, merged, (0, 1))
    block = exchange(local.reshape(cols, part, rows), COL).sum(0)
    left = lax.all_gather(block, COL, axis=0, tiled=True)

    gram_block = dot(block, left, (1, 1))
    shuffled = left.reshape(far, near, step, rows).transpose(1, 0, 2, 3).reshape(rank, rows)
    raw = dot(shuffled, merged, (1, 0)).reshape(near, far * step, width)
    extra = jnp.pad(gram_block, ((0, 0), (0, width - rank)))
    sent = jnp.concatenate([raw, jnp.broadcast_to(extra[None], (near, part, width))], axis=1)
    got = exchange(sent, NEAR_AXIS).sum(0)
    raw = got[: far * step].reshape(far, step, width)
    gram_block = got[far * step :, :rank]
    sent = jnp.concatenate([raw, jnp.broadcast_to(gram_block[None], (far, part, rank))], axis=2)
    got = exchange(sent, FAR_AXIS).sum(0)
    raw_block, gram_block = got[:, :width], got[:, width:]
    gram = exchange(jnp.broadcast_to(gram_block[None], (cols, part, rank)), COL).reshape(rank, rank)
    raw = lax.all_gather(raw_block, (FAR_AXIS, NEAR_AXIS), axis=0, tiled=True)

    chol = jnp.linalg.cholesky(gram)
    inverse = jax.scipy.linalg.solve_triangular(chol, jnp.eye(rank, dtype=jnp.float32), lower=True)
    ortho = dot(inverse, left, (1, 0))
    right = dot(raw, inverse, (0, 1))
    colsq = lax.all_gather(jnp.sum(right * right, axis=0), COL, axis=0).sum(0)
    right_next = right * lax.rsqrt(colsq / full_width + 1e-06)
    new_momentum = merged - 0.05 * dot(ortho, right, (0, 1))
    factor = jnp.sqrt(jnp.float32(depth) / jnp.float32(rank))
    update = (factor * dot(ortho, right_next, (0, 1))).astype(jnp.bfloat16)
    return (new_momentum, right_next, update)


def solution(mesh):
    row, cols = mesh.devices.shape
    far = row // NEAR
    split = Mesh(mesh.devices.reshape(far, NEAR, cols), (FAR_AXIS, NEAR_AXIS, COL))
    both = P((FAR_AXIS, NEAR_AXIS), COL)
    side = P(COL, None)

    def step(momentum, gradient, right_prev):
        return on_device(far, cols, momentum, gradient, right_prev)

    return jax.shard_map(
        step, mesh=split, in_specs=(both, both, side), out_specs=(both, side, both), check_vma=False
    )
```

time: 863 us -> 312 us (0.36)
  waiting for transfers between devices: 688 us -> 33.4 us
  blocking collectives: 83.4 us -> 170 us
  starting transfers between devices: 0.12 us -> 27.6 us
  between operations: 15.2 us -> 2.25 us
    psum x3 -> x0, waiting for transfers between devices: 688 us -> none  [the longest x1 259 us: on_device(): right = lax.psum(local_right, 'row')]
    all_gather x0 -> x3, blocking collectives: none -> 115 us  [the longest x1 54.1 us: on_device(): raw = lax.all_gather(raw_block, (FAR_AXIS, NEAR_AXIS), axis=0, tiled=True)]
    psum x1 -> x0, blocking collectives: 83.4 us -> none  [on_device(): colsq = lax.psum(jnp.sum(right * right, axis=0), 'col')]
    all_to_all x0 -> x2, blocking collectives: none -> 54.3 us  [exchange(): return lax.all_to_all(blocks, axis, 0, 0)]
    all_to_all x0 -> x2, waiting for transfers between devices: none -> 33.4 us  [exchange(): return lax.all_to_all(blocks, axis, 0, 0)]
    all_to_all x0 -> x2, starting transfers between devices: none -> 27.6 us  [exchange(): return lax.all_to_all(blocks, axis, 0, 0)]
  transfers between devices with their start and end apart: 3 -> 2, of which waited for: 3 -> 1; matrix products, arithmetic and copies ran while one was open for 0% -> 0% of each run, Pallas kernels for 0% -> 0%
where the time goes in v1:
time: 312 us; the launch traced here: 311 us
  blocking collectives  170 us (54%)
  other arithmetic  56 us (18%)
  waiting for transfers between devices  33.4 us (11%)
  starting transfers between devices  27.6 us (9%)
  matrix products  14.7 us (5%)
  local copies, waits for them, and re-layouts  7.61 us (2%)
    all_to_all x2, blocking collectives, exchange(): return lax.all_to_all(blocks, axis, 0, 0)  54.3 us
    all_gather x1, blocking collectives, on_device(): raw = lax.all_gather(raw_block, (FAR_AXIS, NEAR_AXIS), axis=0, tiled=True)  54.1 us
    all_gather x1, blocking collectives, on_device(): colsq = lax.all_gather(jnp.sum(right * right, axis=0), COL, axis=0).sum(0)  38 us
    another operation x6, other arithmetic, on_device(): chol = jnp.linalg.cholesky(gram)  33.9 us
    all_to_all x2, waiting for transfers between devices, exchange(): return lax.all_to_all(blocks, axis, 0, 0)  33.4 us
    all_to_all x2, starting transfers between devices, exchange(): return lax.all_to_all(blocks, axis, 0, 0)  27.6 us
    all_gather x1, blocking collectives, on_device(): left = lax.all_gather(block, COL, axis=0, tiled=True)  23.2 us
    another operation x3, other arithmetic, on_device(): jax.scipy.linalg.solve_triangular(chol, jnp.eye(rank, dtype=jnp.float32),...  19.7 us
  transfers between devices with their start and end apart: 2, of which 1 were waited for; matrix products, arithmetic and copies ran while one was open for 0% of the time, Pallas kernels for 0%

profile of v1, /device:TPU:1, one launch (start us, length us, event | category | flops | bytes accessed | tf_op | source)
XLA Modules:
  0.0 311.4 jit_solution(12008456666296983128)
XLA Ops:
  0.6 1.2 copy-done
  1.8 2.9 convolution_bitcast_fusion
  4.7 25.9 %all_to_all.20 = f32[32,8,256]{2,1,0:T(8,128)S(1)} all-to-all(f32[32,8,256]{2,1,0:T(8,128)S(1)} %convolution_bitcast_fusion), channel_id=1, replica_groups=mesh['far'=8,'near'=4,'col'=32] {'col'}, dimensions={0} | all-to-all | bytes 524288 | tf_op jit(solution)/shard_map/all_to_all | solution.py:18
  30.7 23.2 %all_gather.12 = f32[256,256]{1,0:T(8,128)S(1)} all-gather(f32[8,256]{1,0:T(8,128)S(1)} %reduce_sum.45), channel_id=1, replica_groups=mesh['far'=8,'near'=4,'col'=32] {'col'}, dimensions={0}, use_global_device_ids=true | all-gather | bytes 270336 | tf_op jit(solution)/shard_map/all_gather | solution.py:31
  54.2 1.1 fusion.2
  55.4 28.4 %all_to_all.21 = f32[4,72,896]{2,1,0:T(8,128)} all-to-all(f32[4,72,896]{2,1,0:T(8,128)S(1)} %pad_maximum_fusion), channel_id=1, replica_groups=mesh['far'=8,'near'=4,'col'=32] {'near'}, dimensions={0} | all-to-all | bytes 2064384 | tf_op jit(solution)/shard_map/all_to_all | solution.py:18
  83.8 1.3 reduce_sum.46
  85.9 19.6 %all-to-all-start.2 = ((f32[8,8,1152]{2,1,0:T(8,128)}), f32[8,8,1152]{2,1,0:T(8,128)S(1)}, u32[]{:S(2)}, u32[]{:S(2)}) async-start(f32[8,8,1152]{2,1,0:T(8,128)} %pad_maximum_fusion.1), calls=%async_computation.2 | async-start | bytes 589824 | tf_op jit(solution)/shard_map/all_to_all | solution.py:18
  105.5 33.4 %all-to-all-done.2 = f32[8,8,1152]{2,1,0:T(8,128)S(1)} async-done(((f32[8,8,1152]{2,1,0:T(8,128)}), f32[8,8,1152]{2,1,0:T(8,128)S(1)}, u32[]{:S(2)}, u32[]{:S(2)}) %all-to-all-start.2) | async-done | bytes 294944 | tf_op jit(solution)/shard_map/all_to_all | solution.py:18
  140.2 8.1 %all-to-all-start.3 = ((f32[32,8,256]{2,1,0:T(8,128)}), f32[32,8,256]{2,1,0:T(8,128)S(1)}, u32[]{:S(2)}, u32[]{:S(2)}) async-start(f32[32,8,256]{2,1,0:T(8,128)} %broadcast_in_dim.9), calls=%async_computation.3 | async-start | bytes 524288 | tf_op jit(solution)/shard_map/all_to_all | solution.py:18
  148.3 54.1 %all_gather.13 = f32[256,896]{1,0:T(8,128)} all-gather(f32[8,896]{1,0:T(8,128)S(1)} %slice-done), channel_id=1, replica_groups=mesh['far'=8,'near'=4,'col'=32] {'far','near'}, dimensions={0}, use_global_device_ids=true | all-gather | bytes 946176 | tf_op jit(solution)/shard_map/all_gather | solution.py:45
  202.6 11.7 %cholesky.50 = f32[128,128]{1,0:T(8,128)S(1)} custom-call(f32[128,128]{1,0:T(8,128)S(1)} %cholesky.118), custom_call_target="Cholesky" | custom-call | tf_op jit(solution)/shard_map/jit(cholesky)/cholesky | solution.py:47
  214.4 9.8 %custom-call.15 = f32[1,128,128]{1,2,0:T(8,128)S(1)} custom-call(f32[1,128,128]{2,1,0:T(8,128)S(1)} %get-tuple-element.24), custom_call_target="InvertDiagBlocksLowerTriangular" | custom-call | tf_op jit(solution)/shard_map/jit(cholesky)/cholesky | solution.py:47
  224.7 11.7 %cholesky.105 = f32[128,128]{1,0:T(8,128)S(1)} custom-call(f32[128,128]{1,0:T(8,128)S(1)} %convolution_subtract_fusion.1), custom_call_target="Cholesky" | custom-call | tf_op jit(solution)/shard_map/jit(cholesky)/cholesky | solution.py:47
  238.5 4.2 %while.1 = (s32[]{:T(128)}, f32[256,256]{1,0:T(8,128)S(1)}, s32[2,2]{1,0:T(2,128)S(1)}, f32[2,128,128]{2,1,0:T(8,128)S(1)}, s32[]{:T(128)}) while((s32[]{:T(128)}, f32[256,256]{1,0:T(8,128)S(1)}, s32[2,2]{1,0:T(2,128)S(1)}, f32[2,128,128]{2,1,0:T(8,128)S(1)}, s32[]{:T(128)}) %tuple.28), condition=%wide.while_cond, body=%wide.while_body.sunk | while | flops 2 | bytes 131189 | solution.py:48
  239.3 1.4 bitcast_dynamic-update-slice_fusion.2
  241.3 1.4 bitcast_dynamic-update-slice_fusion.2
  242.7 19.7 %custom-call.16 = f32[2,128,128]{1,2,0:T(8,128)S(1)} custom-call(f32[2,128,128]{2,1,0:T(8,128)S(1)} %get-tuple-element.10), custom_call_target="InvertDiagBlocksLowerTriangular" | custom-call | tf_op jit(solution)/shard_map/jit(_solve_triangular)/triangular_solve | solution.py:48
  263.2 1.1 fusion.8
  264.3 2.8 multiply_reduce_fusion
  267.1 38.0 %all-gather.1 = f32[32,1,256]{2,1,0:T(1,128)S(1)} all-gather(f32[1,1,256]{2,1,0:T(1,128)S(1)} %bitcast.60), channel_id=2, replica_groups=mesh['far'=8,'near'=4,'col'=32] {'col'}, dimensions={0}, use_global_device_ids=true | all-gather | bytes 33792 | tf_op jit(solution)/shard_map/all_gather | solution.py:51
  305.2 0.9 copy-done.4
  306.1 2.7 fusion
  308.8 2.6 fusion.1
  (49 shorter events, 6.2 us)
Async XLA Ops:
  0.6 1.2 copy-start
  4.7 49.5 %copy-start.1 = (f32[256,896]{1,0:T(8,128)S(1)}, f32[256,896]{1,0:T(8,128)}, u32[]{:S(2)}) copy-start(f32[256,896]{1,0:T(8,128)} %param.3) | copy-start | bytes 2752516
  30.6 23.6 %copy-start.2 = (bf16[256,896]{1,0:T(8,128)(2,1)S(1)}, bf16[256,896]{1,0:T(8,128)(2,1)}, u32[]{:S(2)}) copy-start(bf16[256,896]{1,0:T(8,128)(2,1)} %param.4) | copy-start | bytes 1376260
  85.9 53.0 %all-to-all-start.2 = ((f32[8,8,1152]{2,1,0:T(8,128)}), f32[8,8,1152]{2,1,0:T(8,128)S(1)}, u32[]{:S(2)}, u32[]{:S(2)}) async-start(f32[8,8,1152]{2,1,0:T(8,128)} %pad_maximum_fusion.1), calls=%async_computation.2 | async-start | bytes 589824 | tf_op jit(solution)/shard_map/all_to_all | solution.py:18
  138.9 0.6 copy-start.5
  140.2 8.1 %slice-start = ((f32[8,1152]{1,0:T(8,128)}), f32[8,896]{1,0:T(8,128)S(1)}, s32[]{:S(2)}) async-start(f32[8,1152]{1,0:T(8,128)} %copy-done.5), calls=%async_computation.4 | async-start | bytes 57344 | tf_op jit(solution)/shard_map/slice | solution.py:43
  140.2 62.2 %all-to-all-start.3 = ((f32[32,8,256]{2,1,0:T(8,128)}), f32[32,8,256]{2,1,0:T(8,128)S(1)}, u32[]{:S(2)}, u32[]{:S(2)}) async-start(f32[32,8,256]{2,1,0:T(8,128)} %broadcast_in_dim.9), calls=%async_computation.3 | async-start | bytes 524288 | tf_op jit(solution)/shard_map/all_to_all | solution.py:18
  305.1 1.0 copy-start.4
  306.1 2.7 copy-start.3

commit v2 on v1

--- a/solution.py
+++ b/solution.py
@@ -1,6 +1,8 @@
 import jax
 import jax.numpy as jnp
 from jax import lax
+from jax.experimental import pallas as pl
+from jax.experimental.pallas import tpu as pltpu
 from jax.sharding import Mesh, PartitionSpec as P
 
 HI = lax.Precision.HIGHEST
@@ -14,8 +16,74 @@
     )
 
 
+def invert64(block):
+    row = lax.broadcasted_iota(jnp.int32, (64, 128), 0)
+    lane = lax.broadcasted_iota(jnp.int32, (64, 128), 1)
+    sub8 = lax.broadcasted_iota(jnp.int32, (8, 128), 0)
+    lane8 = lax.broadcasted_iota(jnp.int32, (8, 128), 1)
+    state = jnp.where(lane < 64, block, jnp.where(lane - 64 == row, 1.0, 0.0))
+
+    def eight(k, state):
+        tile = state[:8]
+        columns = [jnp.broadcast_to(tile[:, i : i + 1], (8, 128)) for i in range(8)]
+        scale = jnp.zeros((8, 128), jnp.float32)
+        for i in range(8):
+            inverse = 1.0 / jnp.broadcast_to(columns[i][i : i + 1], (8, 128))
+            scale = jnp.where(sub8 == i, inverse, scale)
+            factor = jnp.where(sub8 > i, columns[i] * inverse, 0.0)
+            for j in range(i + 1, 8):
+                columns[j] = columns[j] - factor * jnp.broadcast_to(columns[j][i : i + 1], (8, 128))
+            tile = tile - factor * jnp.broadcast_to(tile[i : i + 1], (8, 128))
+        open_lanes = (lane8 >= 8) & (lane8 < 64 - 8 * k)
+        factor = jnp.where(open_lanes, tile * scale, 0.0)[:, :64]
+        rest = state[8:] - dot(factor, tile, (0, 0))[8:]
+        done = tile * jnp.sqrt(scale)
+        return pltpu.roll(jnp.concatenate([rest, done], axis=0), 120, 1)
+
+    state = lax.fori_loop(0, 8, eight, state)
+    return jnp.where(lane < 64, state, 0.0)
+
+
+def tall(x):
+    return jnp.concatenate([x, jnp.zeros_like(x)], axis=0)
+
+
+def invert128(block):
+    first = invert64(block[:64])
+    first_tall = tall(first)
+    below = dot(block[64:], first_tall, (1, 1))
+    rest = pltpu.roll(block[64:], 64, 1) - dot(below, tall(below), (1, 1))
+    second = invert64(rest)
+    corner = dot(second, tall(dot(below, first_tall, (1, 0))), (1, 0))
+    return jnp.concatenate([first, pltpu.roll(second, 64, 1) - corner], axis=0)
+
+
+def invert_kernel(gram_ref, out_ref):
+    first = invert128(gram_ref[:128, :128])
+    below = dot(gram_ref[128:, :128], first, (1, 1))
+    second = invert128(gram_ref[128:, 128:] - dot(below, below, (1, 1)))
+    out_ref[:128, :128] = first
+    out_ref[:128, 128:] = jnp.zeros((128, 128), jnp.float32)
+    out_ref[128:, :128] = -dot(second, dot(below, first, (1, 0)), (1, 0))
+    out_ref[128:, 128:] = second
+
+
+def inverse_factor(gram):
+    return pl.pallas_call(
+        invert_kernel,
+        out_shape=jax.ShapeDtypeStruct((256, 256), jnp.float32),
+        in_specs=[pl.BlockSpec(memory_space=pltpu.VMEM)],
+        out_specs=pl.BlockSpec(memory_space=pltpu.VMEM),
+        cost_estimate=pl.CostEstimate(flops=10_000_000_000, bytes_accessed=50_000_000, transcendentals=0),
+    )(gram)
+
+
 def exchange(blocks, axis):
     return lax.all_to_all(blocks, axis, 0, 0)
+
+
+def collect(block, count, axis):
+    return exchange(jnp.broadcast_to(block[None], (count, *block.shape)), axis)
 
 
 def on_device(far, cols, momentum, gradient, right_prev):
@@ -28,11 +96,10 @@
 
     local = dot(right_prev, merged, (0, 1))
     block = exchange(local.reshape(cols, part, rows), COL).sum(0)
-    left = lax.all_gather(block, COL, axis=0, tiled=True)
+    left = collect(block, cols, COL).reshape(rank, rows)
 
     gram_block = dot(block, left, (1, 1))
-    shuffled = left.reshape(far, near, step, rows).transpose(1, 0, 2, 3).reshape(rank, rows)
-    raw = dot(shuffled, merged, (1, 0)).reshape(near, far * step, width)
+    raw = dot(left, merged, (1, 0)).reshape(near, far * step, width)
     extra = jnp.pad(gram_block, ((0, 0), (0, width - rank)))
     sent = jnp.concatenate([raw, jnp.broadcast_to(extra[None], (near, part, width))], axis=1)
     got = exchange(sent, NEAR_AXIS).sum(0)
@@ -41,14 +108,14 @@
     sent = jnp.concatenate([raw, jnp.broadcast_to(gram_block[None], (far, part, rank))], axis=2)
     got = exchange(sent, FAR_AXIS).sum(0)
     raw_block, gram_block = got[:, :width], got[:, width:]
-    gram = exchange(jnp.broadcast_to(gram_block[None], (cols, part, rank)), COL).reshape(rank, rank)
-    raw = lax.all_gather(raw_block, (FAR_AXIS, NEAR_AXIS), axis=0, tiled=True)
+    gram = lax.all_gather(gram_block, COL, axis=0, tiled=True)
+    raw = collect(raw_block, far, FAR_AXIS).reshape(far * step, width)
+    inverse = inverse_factor(gram)
+    raw = lax.all_gather(raw, NEAR_AXIS, axis=0, tiled=True)
 
-    chol = jnp.linalg.cholesky(gram)
-    inverse = jax.scipy.linalg.solve_triangular(chol, jnp.eye(rank, dtype=jnp.float32), lower=True)
     ortho = dot(inverse, left, (1, 0))
     right = dot(raw, inverse, (0, 1))
-    colsq = lax.all_gather(jnp.sum(right * right, axis=0), COL, axis=0).sum(0)
+    colsq = collect(jnp.sum(right * right, axis=0, keepdims=True), cols, COL).sum(0)
     right_next = right * lax.rsqrt(colsq / full_width + 1e-06)
     new_momentum = merged - 0.05 * dot(ortho, right, (0, 1))
     factor = jnp.sqrt(jnp.float32(depth) / jnp.float32(rank))

time: 312 us -> 226 us (0.72)
  other arithmetic: 56 us -> 1.58 us
  waiting for transfers between devices: 33.4 us -> 4.52 us
  Pallas kernels: 0 us -> 19.4 us
  starting transfers between devices: 27.6 us -> 19.3 us
  blocking collectives: 170 us -> 164 us
  local copies, waits for them, and re-layouts: 7.61 us -> 2.61 us
    all_gather x3 -> x2, blocking collectives: 115 us -> 44.7 us  [the longest x1 25.9 us: on_device(): gram = lax.all_gather(gram_block, COL, axis=0, tiled=True)]
    all_to_all x2 -> x4, blocking collectives: 54.3 us -> 120 us  [exchange(): return lax.all_to_all(blocks, axis, 0, 0)]
    another operation x9 -> x0, other arithmetic: 53.7 us -> none  [the longest x6 33.9 us: on_device(): chol = jnp.linalg.cholesky(gram)]
    all_to_all x2, waiting for transfers between devices: 33.4 us -> 4.52 us  [exchange(): return lax.all_to_all(blocks, axis, 0, 0)]
    pallas_call x0 -> x1, Pallas kernels: none -> 19.4 us  [inverse_factor(): pl.pallas_call(invert_kernel, out_shape=jax.ShapeDtypeStruct((256, 256),...]
    all_to_all x2, starting transfers between devices: 27.6 us -> 19.3 us  [exchange(): return lax.all_to_all(blocks, axis, 0, 0)]
    another operation x9 -> x0, local copies, waits for them, and re-layouts: 4.05 us -> none
  transfers between devices with their start and end apart: 2 -> 2, of which waited for: 1 -> 1; matrix products, arithmetic and copies ran while one was open for 0% -> 2% of each run, Pallas kernels for 0% -> 9%
where the time goes in v2:
time: 226 us; the launch traced here: 225 us
  blocking collectives  164 us (73%)
  Pallas kernels  19.4 us (9%)
  starting transfers between devices  19.3 us (9%)
  matrix products  12.5 us (6%)
  waiting for transfers between devices  4.52 us (2%)
  local copies, waits for them, and re-layouts  2.61 us (1%)
    all_to_all x4, blocking collectives, exchange(): return lax.all_to_all(blocks, axis, 0, 0)  120 us
    all_gather x1, blocking collectives, on_device(): gram = lax.all_gather(gram_block, COL, axis=0, tiled=True)  25.9 us
    pallas_call x1, Pallas kernels, inverse_factor(): pl.pallas_call(invert_kernel, out_shape=jax.ShapeDtypeStruct((256, 256),...  19.4 us
    all_to_all x2, starting transfers between devices, exchange(): return lax.all_to_all(blocks, axis, 0, 0)  19.3 us
    all_gather x1, blocking collectives, on_device(): raw = lax.all_gather(raw, NEAR_AXIS, axis=0, tiled=True)  18.8 us
    dot_general x7, matrix products, dot(): lax.dot_general(a, b, ((contract[:1], contract[1:]), ((), ())), precision...  12.5 us
  transfers between devices with their start and end apart: 2, of which 1 were waited for; matrix products, arithmetic and copies ran while one was open for 2% of the time, Pallas kernels for 9%

profile of v2, /device:TPU:1, one launch (start us, length us, event | category | flops | bytes accessed | tf_op | source)
XLA Modules:
  0.0 225.1 jit_solution(5507453128082937047)
XLA Ops:
  0.6 1.2 copy-done
  1.8 2.9 %convolution_bitcast_fusion = f32[32,8,256]{2,1,0:T(8,128)S(1)} fusion(f32[896,256]{1,0:T(8,128)S(1)} %copy-done, f32[256,896]{1,0:T(8,128)} %param.3, bf16[256,896]{1,0:T(8,128)(2,1)} %param.4), kind=kOutput, calls=%fused_computation.4 | convolution fusion | flops 705101824 | bytes 2555904 | tf_op jit(solution)/shard_map/dot_general | solution.py:14
  4.7 25.9 %all_to_all.30 = f32[32,8,256]{2,1,0:T(8,128)S(1)} all-to-all(f32[32,8,256]{2,1,0:T(8,128)S(1)} %convolution_bitcast_fusion), channel_id=1, replica_groups=mesh['far'=8,'near'=4,'col'=32] {'col'}, dimensions={0} | all-to-all | bytes 524288 | tf_op jit(solution)/shard_map/all_to_all | solution.py:82
  30.7 12.6 %all_to_all.31 = f32[32,8,256]{2,1,0:T(8,128)S(1)} all-to-all(f32[32,8,256]{2,1,0:T(8,128)S(1)} %broadcast_in_dim.10), channel_id=1, replica_groups=mesh['far'=8,'near'=4,'col'=32] {'col'}, dimensions={0} | all-to-all | bytes 524288 | tf_op jit(solution)/shard_map/all_to_all | solution.py:82
  43.3 0.3 fusion.6
  43.6 1.1 fusion.2
  44.7 0.1 pad_maximum_fusion
  44.7 28.4 %all_to_all.32 = f32[4,72,896]{2,1,0:T(8,128)} all-to-all(f32[4,72,896]{2,1,0:T(8,128)S(1)} %pad_maximum_fusion), channel_id=1, replica_groups=mesh['far'=8,'near'=4,'col'=32] {'near'}, dimensions={0} | all-to-all | bytes 2064384 | tf_op jit(solution)/shard_map/all_to_all | solution.py:82
  73.2 1.3 reduce_sum.46
  74.6 52.8 %all_to_all.33 = f32[8,8,1152]{2,1,0:T(8,128)S(1)} all-to-all(f32[8,8,1152]{2,1,0:T(8,128)S(1)} %pad_maximum_fusion.1), channel_id=1, replica_groups=mesh['far'=8,'near'=4,'col'=32] {'far'}, dimensions={0} | all-to-all | bytes 589824 | tf_op jit(solution)/shard_map/all_to_all | solution.py:82
  127.4 0.7 broadcast_in_dim.13
  128.1 13.8 %all-to-all-start.4 = ((f32[8,8,896]{2,1,0:T(8,128)}), f32[8,8,896]{2,1,0:T(8,128)S(1)}, u32[]{:S(2)}, u32[]{:S(2)}) async-start(f32[8,8,896]{2,1,0:T(8,128)} %broadcast_in_dim.13), calls=%async_computation.4 | async-start | bytes 458752 | tf_op jit(solution)/shard_map/all_to_all | solution.py:82
  141.9 25.9 %all_gather.6.gram_ref = f32[256,256]{1,0:T(8,128)} all-gather(f32[8,256]{1,0:T(8,128)S(1)} %slice.18), channel_id=1, replica_groups=mesh['far'=8,'near'=4,'col'=32] {'col'}, dimensions={0}, use_global_device_ids=true | all-gather | bytes 270336 | tf_op jit(solution)/shard_map/all_gather | solution.py:111
  167.8 19.4 %shard_map.58 = f32[256,256]{1,0:T(8,128)} custom-call(f32[256,256]{1,0:T(8,128)} %all_gather.6.gram_ref), custom_call_target="tpu_custom_call" | custom-call | flops 10000000000 | bytes 50000000 | tf_op jit(solution)/shard_map/pallas_call | solution.py:72
  187.2 1.3 fusion.4
  188.5 18.8 %all_gather.7 = f32[256,896]{1,0:T(8,128)S(1)} all-gather(f32[64,896]{1,0:T(8,128)S(1)} %bitcast.27), channel_id=1, replica_groups=mesh['far'=8,'near'=4,'col'=32] {'near'}, dimensions={0}, use_global_device_ids=true | all-gather | bytes 1146880 | tf_op jit(solution)/shard_map/all_gather | solution.py:114
  207.3 1.6 multiply_reduce_fusion
  208.9 0.6 broadcast_in_dim.14
  209.6 5.5 %all-to-all-start.5 = ((f32[32,1,256]{2,1,0:T(1,128)}), f32[32,1,256]{2,1,0:T(1,128)S(1)}, u32[]{:S(2)}, u32[]{:S(2)}) async-start(f32[32,1,256]{2,1,0:T(1,128)} %broadcast_in_dim.14), calls=%async_computation.5 | async-start | bytes 65536 | tf_op jit(solution)/shard_map/all_to_all | solution.py:82
  215.1 2.7 %fusion = f32[256,896]{1,0:T(8,128)} fusion(f32[256,256]{1,0:T(8,128)S(1)} %fusion.4, f32[896,256]{1,0:T(8,128)S(1)} %get-tuple-element.4, f32[256,896]{1,0:T(8,128)S(1)} %copy-done.1, bf16[256,896]{1,0:T(8,128)(2,1)S(1)} %copy-done.2), kind=kOutput, calls=%fused_computation.2 | convolution fusion | flops 705560576 | bytes 3473408 | tf_op jit(solution)/shard_map/dot_general | solution.py:14
  217.9 4.5 %all-to-all-done.5 = f32[32,1,256]{2,1,0:T(1,128)S(1)} async-done(((f32[32,1,256]{2,1,0:T(1,128)}), f32[32,1,256]{2,1,0:T(1,128)S(1)}, u32[]{:S(2)}, u32[]{:S(2)}) %all-to-all-start.5) | async-done | bytes 32800 | tf_op jit(solution)/shard_map/all_to_all | solution.py:82
  222.4 0.1 reduce_sum.49
  222.4 0.1 broadcast_multiply_fusion
  222.5 2.6 %fusion.1 = bf16[256,896]{1,0:T(8,128)(2,1)} fusion(f32[256,256]{1,0:T(8,128)S(1)} %fusion.4, f32[896,256]{1,0:T(8,128)S(1)} %broadcast_multiply_fusion), kind=kOutput, calls=%fused_computation.3 | convolution fusion | flops 705101824 | bytes 1638400 | tf_op jit(solution)/shard_map/dot_general | solution.py:14
  (22 shorter events, 0.2 us)
Async XLA Ops:
  0.6 1.2 copy-start
  4.7 38.8 %copy-start.1 = (f32[256,896]{1,0:T(8,128)S(1)}, f32[256,896]{1,0:T(8,128)}, u32[]{:S(2)}) copy-start(f32[256,896]{1,0:T(8,128)} %param.3) | copy-start | bytes 2752516
  30.7 12.9 %copy-start.2 = (bf16[256,896]{1,0:T(8,128)(2,1)S(1)}, bf16[256,896]{1,0:T(8,128)(2,1)}, u32[]{:S(2)}) copy-start(bf16[256,896]{1,0:T(8,128)(2,1)} %param.4) | copy-start | bytes 1376260
  128.1 60.4 %all-to-all-start.4 = ((f32[8,8,896]{2,1,0:T(8,128)}), f32[8,8,896]{2,1,0:T(8,128)S(1)}, u32[]{:S(2)}, u32[]{:S(2)}) async-start(f32[8,8,896]{2,1,0:T(8,128)} %broadcast_in_dim.13), calls=%async_computation.4 | async-start | bytes 458752 | tf_op jit(solution)/shard_map/all_to_all | solution.py:82
  188.5 18.8 %copy-start.4 = (f32[256,256]{1,0:T(8,128)S(1)}, f32[256,256]{1,0:T(8,128)}, u32[]{:S(2)}) copy-start(f32[256,256]{1,0:T(8,128)} %shard_map.58) | copy-start | bytes 786436
  209.6 12.8 %all-to-all-start.5 = ((f32[32,1,256]{2,1,0:T(1,128)}), f32[32,1,256]{2,1,0:T(1,128)S(1)}, u32[]{:S(2)}, u32[]{:S(2)}) async-start(f32[32,1,256]{2,1,0:T(1,128)} %broadcast_in_dim.14), calls=%async_computation.5 | async-start | bytes 65536 | tf_op jit(solution)/shard_map/all_to_all | solution.py:82
  222.5 2.6 %copy-start.3 = (f32[896,256]{1,0:T(8,128)}, f32[896,256]{1,0:T(8,128)S(1)}, u32[]{:S(2)}) copy-start(f32[896,256]{1,0:T(8,128)S(1)} %broadcast_multiply_fusion) | copy-start | bytes 2752516
